TPU v7x, 32 devices: a whole 2x2x4 slice. The times are simulated.
32 devices in a mesh: section: 2 (over core), replica: 16 (over z, y, x).
Axes of the slice: x: 2, y: 2, z: 4, core: 2. Of those that a mesh axis runs over, the one named last changes fastest.
Arguments:
- tokens: bfloat16 [16, 2, 128, 1536], P('replica'), may hold values from -6 to 6
- cotangent: bfloat16 [16, 2, 128, 1536], P('replica'), may hold values from -6 to 6
- block_lengths: int32 [16, 2, 4], P('replica'), may hold values from 1 to 48, 128 in all within a row
- weights: bfloat16 [2, 16, 1536, 768], P('section', 'replica'), may hold values from -0.15625 to 0.15625
- momentum: bfloat16 [2, 16, 1536, 768], P('section', 'replica'), may hold values from -60 to 60
- step_index: int32 [1], replicated, may hold values from 0 to 63
Outputs:
- new_weights: bfloat16 [2, 16, 1536, 768], P('section', 'replica')
- new_momentum: bfloat16 [2, 16, 1536, 768], P('section', 'replica')
Inputs may be any that keep to these rules, and one draw needn't show every extreme that they name: `block_lengths`: each micro-batch's 4 block lengths sum to 128.
All inputs are finite; a program needn't handle non-finite values.
Results may differ from a plain program's by a relative error of at most 0.009.
Values may be sent and summed in bfloat16 or wider, within the bound.
A program may use at most 64 MiB of HBM per device.

v0:
```python
from functools import partial

import jax
import jax.numpy as jnp
from jax import lax
from jax.experimental import pallas as pl
from jax.experimental.pallas import tpu as pltpu
from jax.sharding import PartitionSpec as P

HS = 128
SHARES = (5, 4, 2, 1)


F32 = jnp.float32
BF16 = jnp.bfloat16
NT = (((1,), (1,)), ((), ()))
TN = (((0,), (0,)), ((), ()))
NN = (((1,), (0,)), ((), ()))


def mm(a, b, dims=NN):
    return lax.dot_general(a, b, dims, preferred_element_type=F32)


def visible(lengths_ref, micro, rows):
    q_at = lax.broadcasted_iota(jnp.int32, (rows, rows), 0)
    k_at = lax.broadcasted_iota(jnp.int32, (rows, rows), 1)
    q_id = jnp.zeros((rows, rows), jnp.int32)
    k_id = jnp.zeros((rows, rows), jnp.int32)
    bound = jnp.int32(0)
    for block in range(lengths_ref.shape[1]):
        bound = bound + lengths_ref[micro, block]
        q_id = q_id + (q_at >= bound).astype(jnp.int32)
        k_id = k_id + (k_at >= bound).astype(jnp.int32)
    return k_id <= q_id


def normalize(x_ref, n_ref):
    def rows(r):
        xf = x_ref[r, :].astype(F32)
        scale = lax.rsqrt(jnp.mean(xf * xf, axis=1, keepdims=True) + 1e-06)
        n_ref[r, :] = (xf * scale).astype(BF16)

    each_block(x_ref.shape[0], 32, rows)


def weights_of(u_head, vis):
    raised = jnp.where(vis, jnp.exp(mm(u_head, u_head, NT) * (1.0 / HS)), 0.0)
    return raised / jnp.sum(raised, axis=1, keepdims=True)


def block_of(extent):
    return 256 if extent % 256 == 0 else HS


def each_block(extent, size, body):
    def once(index, carry):
        body(pl.ds(pl.multiple_of(index * size, size), size))
        return carry

    lax.fori_loop(0, extent // size, once, 0)


def project(out_ref, left_ref, w_ref):
    def body(c):
        out_ref[:, c] = mm(left_ref[...], w_ref[:, c]).astype(BF16)

    each_block(w_ref.shape[1], block_of(w_ref.shape[1]), body)


def each_head(lengths_ref, rows_all, width, body):
    micros = lengths_ref.shape[0]
    rows = rows_all // micros
    masks = [visible(lengths_ref, micro, rows) for micro in range(micros)]

    def heads(c):
        for micro in range(micros):
            body(slice(micro * rows, (micro + 1) * rows), c, masks[micro])

    each_block(width, HS, heads)


def forward_kernel(lengths_ref, x_ref, w_ref, out_ref, n_ref, u_ref, a_ref):
    normalize(x_ref, n_ref)
    project(u_ref, n_ref, w_ref)

    def head(r, c, mask):
        uh = u_ref[r, c]
        a_ref[r, c] = mm(weights_of(uh, mask).astype(BF16), uh).astype(BF16)

    each_head(lengths_ref, x_ref.shape[0], w_ref.shape[1], head)

    def body(c):
        out = x_ref[:, c].astype(F32) + mm(a_ref[...], w_ref[c, :], NT)
        out_ref[:, c] = out.astype(BF16)

    each_block(w_ref.shape[0], block_of(w_ref.shape[0]), body)


def attention_back(lengths_ref, n_ref, d_ref, w_ref, u_ref, da_ref, du_ref, a_ref):
    project(u_ref, n_ref, w_ref)
    project(da_ref, d_ref, w_ref)

    def head(r, c, mask):
        uh, dah = u_ref[r, c], da_ref[r, c]
        p = weights_of(uh, mask)
        pb = p.astype(BF16)
        if a_ref is not None:
            a_ref[r, c] = mm(pb, uh).astype(BF16)
        dp = mm(dah, uh, NT)
        ds = (p * (dp - jnp.sum(dp * p, axis=1, keepdims=True)) * (1.0 / HS)).astype(BF16)
        du = mm(pb, dah, TN) + mm(ds, uh) + mm(ds, uh, TN)
        du_ref[r, c] = du.astype(BF16)

    each_head(lengths_ref, d_ref.shape[0], w_ref.shape[1], head)


def input_grad_kernel(lengths_ref, x_ref, d_ref, w_ref, out_ref, n_ref, u_ref, da_ref, du_ref, dn_ref):
    normalize(x_ref, n_ref)
    attention_back(lengths_ref, n_ref, d_ref, w_ref, u_ref, da_ref, du_ref, None)

    def body(c):
        dn_ref[:, c] = mm(du_ref[...], w_ref[c, :], NT)

    each_block(w_ref.shape[0], block_of(w_ref.shape[0]), body)

    def rows(r):
        xf = x_ref[r, :].astype(F32)
        dn = dn_ref[r, :]
        scale = lax.rsqrt(jnp.mean(xf * xf, axis=1, keepdims=True) + 1e-06)
        along = jnp.mean(dn * xf, axis=1, keepdims=True)
        dx = scale * dn - xf * (scale * scale * scale * along)
        out_ref[r, :] = (d_ref[r, :].astype(F32) + dx).astype(BF16)

    each_block(x_ref.shape[0], 32, rows)


def local_kernel(lengths_ref, x_ref, d_ref, w_ref, m_ref, *rest):
    out_refs, (n_ref, u_ref, da_ref, du_ref, a_ref) = rest[:-5], rest[-5:]
    normalize(x_ref, n_ref)
    attention_back(lengths_ref, n_ref, d_ref, w_ref, u_ref, da_ref, du_ref, a_ref)
    start = 0
    for out_ref in out_refs:

        def once(index, carry, start=start, out_ref=out_ref):
            c = pl.ds(pl.multiple_of(start + index * HS, HS), HS)
            r = pl.ds(pl.multiple_of(index * HS, HS), HS)
            grad = mm(n_ref[:, c], du_ref[...], TN) + mm(d_ref[:, c], a_ref[...], TN)
            out_ref[r, :] = (0.9 * m_ref[c, :].astype(F32) + grad).astype(BF16)
            return carry

        lax.fori_loop(0, out_ref.shape[0] // HS, once, 0)
        start += out_ref.shape[0]


def combine_kernel(l_ref, lp_ref, w_ref, wp_ref, *rest):
    nw_ref, nm_ref = rest[-2:]
    average = 0.5 * (l_ref[...].astype(F32) + lp_ref[...].astype(F32))
    weight = 0.5 * (w_ref[...].astype(F32) + wp_ref[...].astype(F32))
    nm_ref[...] = average.astype(BF16)
    nw_ref[...] = (weight - 0.0005 * average).astype(BF16)


def vmem(count):
    return [pl.BlockSpec(memory_space=pltpu.VMEM)] * count


SMEM = [pl.BlockSpec(memory_space=pltpu.SMEM)]


def cost(flops, bytes_moved, exps):
    return pl.CostEstimate(flops=flops, bytes_accessed=bytes_moved, transcendentals=exps)


def scratch(x, width, count):
    return [pltpu.VMEM(x.shape, BF16)] + [pltpu.VMEM((x.shape[0], width), BF16)] * count


def sizes_of(total):
    unit = total // sum(SHARES)
    return [share * unit for share in SHARES]


def run_forward(lengths, x, w):
    rows, width = x.shape[0], w.shape[1]
    return pl.pallas_call(
        forward_kernel,
        out_shape=jax.ShapeDtypeStruct(x.shape, BF16),
        in_specs=SMEM + vmem(2),
        out_specs=vmem(1)[0],
        scratch_shapes=scratch(x, width, 2),
        cost_estimate=cost(4 * rows * w.size, 2 * (w.size + 2 * x.size), rows * width),
        name="section_forward",
    )(lengths, x, w)


def run_input_grad(lengths, x, d, w):
    rows, width = x.shape[0], w.shape[1]
    return pl.pallas_call(
        input_grad_kernel,
        out_shape=jax.ShapeDtypeStruct(x.shape, BF16),
        in_specs=SMEM + vmem(3),
        out_specs=vmem(1)[0],
        scratch_shapes=scratch(x, width, 3) + [pltpu.VMEM(x.shape, F32)],
        cost_estimate=cost(6 * rows * w.size, 2 * (w.size + 3 * x.size), rows * width),
        name="section_input_grad",
    )(lengths, x, d, w)


def run_local(lengths, x, d, w, m):
    rows, width = x.shape[0], w.shape[1]
    sizes = sizes_of(w.shape[0])
    return pl.pallas_call(
        local_kernel,
        out_shape=[jax.ShapeDtypeStruct((size, width), BF16) for size in sizes],
        in_specs=SMEM + vmem(4),
        out_specs=vmem(len(sizes)),
        scratch_shapes=scratch(x, width, 4),
        cost_estimate=cost(8 * rows * w.size, 2 * (3 * w.size + 2 * x.size), rows * width),
        name="section_local",
    )(lengths, x, d, w, m)


def run_combine(start, mine, theirs, w, wp, filled):
    size, width = mine.shape
    block = HS
    first = start // block
    own = pl.BlockSpec((block, width), lambda i: (i, 0))
    within = pl.BlockSpec((block, width), lambda i: (first + i, 0))
    whole = jax.ShapeDtypeStruct(w.shape, BF16)
    return pl.pallas_call(
        combine_kernel,
        out_shape=[whole, whole],
        grid=(size // block,),
        in_specs=[own, own, within, within] + [pl.BlockSpec(memory_space=pl.ANY)] * len(filled),
        out_specs=[within, within],
        input_output_aliases={4 + i: i for i in range(len(filled))},
        cost_estimate=cost(8 * mine.size, 12 * mine.size, 0),
        name="combine",
    )(mine, theirs, w, wp, *filled)


def partner(value, axis, stride):
    mask = 2**stride
    pairs = [(source, source ^ mask) for source in range(lax.axis_size(axis))]
    return lax.ppermute(value, axis, pairs)


def shifted(value, axis, steps):
    count = lax.axis_size(axis)
    leading, last = (max(0, -steps), min(count, count - steps))
    return lax.ppermute(value, axis, [(source, source + steps) for source in range(leading, last)])


def step(bit, tokens, cotangent, lengths, weight, momentum):
    sections = lax.axis_size("section")
    here = lax.axis_index("section")
    theirs = partner(weight, "replica", bit)
    x, d = tokens, cotangent
    for tick in range(sections - 1):
        leaving = run_forward(lengths, x, weight)
        arriving = shifted(leaving, "section", 1)
        x = jnp.where(here == tick + 1, arriving, x)
    for tick in range(sections - 1):
        arriving = shifted(run_input_grad(lengths, x, d, weight), "section", -1)
        d = jnp.where(here == sections - 2 - tick, arriving, d)
    pieces = run_local(lengths, x, d, weight, momentum)
    others = [partner(piece, "replica", bit) for piece in pieces]
    filled, start = (), 0
    for mine, other in zip(pieces[:-1], others[:-1]):
        filled = run_combine(start, mine, other, weight, theirs, filled)
        start += mine.shape[0]
    return (*filled, pieces[-1], others[-1], theirs)


def per_device(tokens, cotangent, block_lengths, weights, momentum, step_index):
    rows = tokens.shape[1] * tokens.shape[2]
    wide = tokens.shape[3]
    weight = weights[0, 0]
    *filled, mine, other, theirs = lax.switch(
        step_index[0] % 4,
        [partial(step, bit) for bit in range(4)],
        tokens.reshape(rows, wide),
        cotangent.reshape(rows, wide),
        block_lengths[0],
        weight,
        momentum[0, 0],
    )
    new_weight, new_momentum = run_combine(
        weight.shape[0] - mine.shape[0], mine, other, weight, theirs, filled
    )
    return new_weight[None, None], new_momentum[None, None]


def solution(mesh):
    in_specs = (
        P("replica", None, None, None),
        P("replica", None, None, None),
        P("replica", None, None),
        P("section", "replica", None, None),
        P("section", "replica", None, None),
        P(),
    )
    out_specs = (P("section", "replica", None, None), P("section", "replica", None, None))
    return jax.shard_map(
        per_device, mesh=mesh, in_specs=in_specs, out_specs=out_specs, check_vma=False
    )
```

profile of v0, /device:TPU:0, one launch (start us, length us, event | category | flops | bytes accessed | tf_op | source)
XLA Modules:
  0.0 138.3 jit_solution(15455979159446912855)
XLA Ops:
  1.3 134.9 %conditional.1 = (bf16[1536,768]{1,0:T(8,128)(2,1)}, bf16[1536,768]{1,0:T(8,128)(2,1)}, bf16[128,768]{1,0:T(8,128)(2,1)}, bf16[128,768]{1,0:T(8,128)(2,1)}, bf16[1536,768]{1,0:T(8,128)(2,1)}) conditional(s32[]{:T(128)} %clamp.3, (s32[2,4]{1,0:T(2,128)}, bf16[256,1536]{1,0:T(8,128)(2,1)}, bf16[1536,768]{1,0:T(8,128)(2,1)}, ...), branch_computations={%region_0.1_spmd, %region_1.2_spmd, %region_2.3_spmd, %region_3.4_... | conditional | flops 5445255168 | bytes 79823488 | solution.py:280
  1.4 10.6 %section_forward.6 = bf16[256,1536]{1,0:T(8,128)(2,1)} custom-call(s32[2,4]{1,0:T(2,128)} %get-tuple-element.70.lengths_ref, bf16[256,1536]{1,0:T(8,128)(2,1)} %get-tuple-element.71.x_ref, bf16[1536,768]{1,0:T(8,128)(2,1)} %get-tuple-element.72.w_ref), custom_call_target="tpu_custom_call" | custom-call | flops 1207959552 | bytes 3932160 | tf_op jit(solution)/shard_map/cond/branch_2_fun/section_forward/pallas_call | solution.py:186
  11.9 3.3 %collective-permute-start.14 = (bf16[256,1536]{1,0:T(8,128)(2,1)}, bf16[256,1536]{1,0:T(8,128)(2,1)}, u32[]{:S(2)}, u32[]{:S(2)}) collective-permute-start(bf16[256,1536]{1,0:T(8,128)(2,1)} %section_forward.6), channel_id=1, source_target_pairs={{0,16},{1,17},{2,18},{3,19},{4,20},{5,21},{6,22},{7,23},{8,24},{9,... | collective-permute-start | bytes 2359304 | tf_op jit(solution)/shard_map/cond/branch_2_fun/ppermute | solution.py:252
  15.2 1.3 collective-permute-done.14
  16.6 1.0 broadcast_select_fusion.5.x_ref
  17.5 13.8 %section_input_grad.6 = bf16[256,1536]{1,0:T(8,128)(2,1)} custom-call(s32[2,4]{1,0:T(2,128)S(1)} %copy-done.18, bf16[256,1536]{1,0:T(8,128)(2,1)} %broadcast_select_fusion.5.x_ref, bf16[256,1536]{1,0:T(8,128)(2,1)} %get-tuple-element.73.d_ref, bf16[1536,768]{1,0:T(8,128)(2,1)S(1)} %copy-done.2), custom_call_target="tpu_custom_call" | custom-call | flops 1811939328 | bytes 4718592 | tf_op jit(solution)/shard_map/cond/branch_2_fun/section_input_grad/pallas_call | solution.py:199
  31.4 1.3 collective-permute-start.15
  32.6 2.5 %collective-permute-start.17 = (bf16[1536,768]{1,0:T(8,128)(2,1)S(1)}, bf16[1536,768]{1,0:T(8,128)(2,1)}, u32[]{:S(2)}, u32[]{:S(2)}) collective-permute-start(bf16[1536,768]{1,0:T(8,128)(2,1)S(1)} %copy-done.2), channel_id=1, source_target_pairs={{0,4},{1,5},{2,6},{3,7},{4,0},{5,1},{6,2},{7,3},{8,12},{9,13},{10,... | collective-permute-start | bytes 7077896 | tf_op jit(solution)/shard_map/cond/branch_2_fun/ppermute | solution.py:246
  35.1 1.1 collective-permute-done.15
  36.2 2.1 %broadcast_select_fusion.4.d_ref = bf16[256,1536]{1,0:T(8,128)(2,1)} fusion(bf16[256,1536]{1,0:T(8,128)(2,1)} %collective-permute-done.15, bf16[256,1536]{1,0:T(8,128)(2,1)S(1)} %copy-done.10, pred[]{:T(512)S(6)} %eq.23), kind=kLoop, calls=%fused_computation.4 | loop fusion | flops 393216 | bytes 2359297 | tf_op jit(solution)/shard_map/cond/branch_2_fun/jit(_where)/select_n | solution.py:266
  38.3 15.8 %section_local.6 = (bf16[640,768]{1,0:T(8,128)(2,1)}, bf16[512,768]{1,0:T(8,128)(2,1)}, bf16[256,768]{1,0:T(8,128)(2,1)}, bf16[128,768]{1,0:T(8,128)(2,1)}) custom-call(s32[2,4]{1,0:T(2,128)S(1)} %copy-done.18, bf16[256,1536]{1,0:T(8,128)(2,1)} %broadcast_select_fusion.5.x_ref, bf16[256,1536]{1,0:T(8,128)(2,1)} %broadcast_select_fusion.4.d_ref, ...), custom_call_target="tpu_custom_call" | custom-call | flops 2415919104 | bytes 8650752 | tf_op jit(solution)/shard_map/cond/branch_2_fun/section_local/pallas_call | solution.py:213
  54.1 2.4 %collective-permute-start.19 = (bf16[640,768]{1,0:T(8,128)(2,1)}, bf16[640,768]{1,0:T(8,128)(2,1)S(1)}, u32[]{:S(2)}, u32[]{:S(2)}) collective-permute-start(bf16[640,768]{1,0:T(8,128)(2,1)} %get-tuple-element.77.l_ref), channel_id=1, source_target_pairs={{0,4},{1,5},{2,6},{3,7},{4,0},{5,1},{6,2},{7,3},{8,12},{9,13},{10,... | collective-permute-start | bytes 2949128 | tf_op jit(solution)/shard_map/cond/branch_2_fun/ppermute | solution.py:246
  56.5 0.0 collective-permute-start.18
  56.6 2.0 %collective-permute-start.16 = (bf16[256,768]{1,0:T(8,128)(2,1)}, bf16[256,768]{1,0:T(8,128)(2,1)}, u32[]{:S(2)}, u32[]{:S(2)}) collective-permute-start(bf16[256,768]{1,0:T(8,128)(2,1)} %get-tuple-element.75.l_ref), channel_id=1, source_target_pairs={{0,4},{1,5},{2,6},{3,7},{4,0},{5,1},{6,2},{7,3},{8,12},{9,13},{10,... | collective-permute-start | bytes 1179656 | tf_op jit(solution)/shard_map/cond/branch_2_fun/ppermute | solution.py:246
  58.6 27.1 %collective-permute-done.17.wp_ref = bf16[1536,768]{1,0:T(8,128)(2,1)} collective-permute-done((bf16[1536,768]{1,0:T(8,128)(2,1)S(1)}, bf16[1536,768]{1,0:T(8,128)(2,1)}, u32[]{:S(2)}, u32[]{:S(2)}) %collective-permute-start.17) | collective-permute-done | bytes 2359328 | tf_op jit(solution)/shard_map/cond/branch_2_fun/ppermute | solution.py:246
  85.7 21.0 %collective-permute-done.19.lp_ref = bf16[640,768]{1,0:T(8,128)(2,1)S(1)} collective-permute-done((bf16[640,768]{1,0:T(8,128)(2,1)}, bf16[640,768]{1,0:T(8,128)(2,1)S(1)}, u32[]{:S(2)}, u32[]{:S(2)}) %collective-permute-start.19) | collective-permute-done | bytes 983072 | tf_op jit(solution)/shard_map/cond/branch_2_fun/ppermute | solution.py:246
  106.6 0.9 copy-done.14
  107.6 4.8 %combine.19 = (bf16[1536,768]{1,0:T(8,128)(2,1)}, bf16[1536,768]{1,0:T(8,128)(2,1)}) custom-call(bf16[640,768]{1,0:T(8,128)(2,1)} %get-tuple-element.77.l_ref, bf16[640,768]{1,0:T(8,128)(2,1)} %copy-done.14, bf16[1536,768]{1,0:T(8,128)(2,1)S(1)} %copy-done.2, bf16[1536,768]{1,0:T(8,128)(2,1)} %collective-permute-done.17.wp_ref), custom_call_target="tpu_custom_call" | custom-call | flops 3932160 | bytes 5898240 | tf_op jit(solution)/shard_map/cond/branch_2_fun/combine/pallas_call | solution.py:231
  112.4 11.2 %collective-permute-done.18.lp_ref = bf16[512,768]{1,0:T(8,128)(2,1)} collective-permute-done((bf16[512,768]{1,0:T(8,128)(2,1)}, bf16[512,768]{1,0:T(8,128)(2,1)}, u32[]{:S(2)}, u32[]{:S(2)}) %collective-permute-start.18) | collective-permute-done | bytes 786464 | tf_op jit(solution)/shard_map/cond/branch_2_fun/ppermute | solution.py:246
  123.6 3.9 %combine.20 = (bf16[1536,768]{1,0:T(8,128)(2,1)}, bf16[1536,768]{1,0:T(8,128)(2,1)}) custom-call(bf16[512,768]{1,0:T(8,128)(2,1)} %get-tuple-element.76.l_ref, bf16[512,768]{1,0:T(8,128)(2,1)} %collective-permute-done.18.lp_ref, bf16[1536,768]{1,0:T(8,128)(2,1)S(1)} %copy-done.2, ...), custom_call_target="tpu_custom_call", output_to_operand_aliasing={{0}: (4, {}), {1}: (5, {})} | custom-call | flops 3145728 | bytes 4718592 | tf_op jit(solution)/shard_map/cond/branch_2_fun/combine/pallas_call | solution.py:231
  127.5 4.5 %collective-permute-done.16.lp_ref = bf16[256,768]{1,0:T(8,128)(2,1)} collective-permute-done((bf16[256,768]{1,0:T(8,128)(2,1)}, bf16[256,768]{1,0:T(8,128)(2,1)}, u32[]{:S(2)}, u32[]{:S(2)}) %collective-permute-start.16) | collective-permute-done | bytes 393248 | tf_op jit(solution)/shard_map/cond/branch_2_fun/ppermute | solution.py:246
  132.0 2.2 %combine.21 = (bf16[1536,768]{1,0:T(8,128)(2,1)}, bf16[1536,768]{1,0:T(8,128)(2,1)}) custom-call(bf16[256,768]{1,0:T(8,128)(2,1)} %get-tuple-element.75.l_ref, bf16[256,768]{1,0:T(8,128)(2,1)} %collective-permute-done.16.lp_ref, bf16[1536,768]{1,0:T(8,128)(2,1)S(1)} %copy-done.2, ...), custom_call_target="tpu_custom_call", output_to_operand_aliasing={{0}: (4, {}), {1}: (5, {})} | custom-call | flops 1572864 | bytes 2359296 | tf_op jit(solution)/shard_map/cond/branch_2_fun/combine/pallas_call | solution.py:231
  134.2 2.0 %collective-permute-done.20 = bf16[128,768]{1,0:T(8,128)(2,1)} collective-permute-done((bf16[128,768]{1,0:T(8,128)(2,1)}, bf16[128,768]{1,0:T(8,128)(2,1)}, u32[]{:S(2)}, u32[]{:S(2)}) %collective-permute-start.20) | collective-permute-done | bytes 196640 | tf_op jit(solution)/shard_map/cond/branch_2_fun/ppermute | solution.py:246
  136.2 2.1 %combine.25 = (bf16[1536,768]{1,0:T(8,128)(2,1)}, bf16[1536,768]{1,0:T(8,128)(2,1)}) custom-call(bf16[128,768]{1,0:T(8,128)(2,1)} %get-tuple-element.109.l_ref, bf16[128,768]{1,0:T(8,128)(2,1)} %get-tuple-element.110.lp_ref, bf16[1536,768]{1,0:T(8,128)(2,1)} %bitcast.15, ...), custom_call_target="tpu_custom_call", output_to_operand_aliasing={{0}: (4, {}), {1}: (5, {})} | custom-call | flops 786432 | bytes 1179648 | tf_op jit(solution)/shard_map/combine/pallas_call | solution.py:231
  (10 shorter events, 0.0 us)
Async XLA Ops:
  1.3 15.2 %copy-start.6 = (bf16[256,1536]{1,0:T(8,128)(2,1)S(1)}, bf16[256,1536]{1,0:T(8,128)(2,1)}, u32[]{:S(2)}) copy-start(bf16[256,1536]{1,0:T(8,128)(2,1)} %get-tuple-element.71.x_ref) | copy-start | bytes 2359300 | tf_op jit(solution)/shard_map/cond
  1.3 16.2 %copy-start.2 = (bf16[1536,768]{1,0:T(8,128)(2,1)S(1)}, bf16[1536,768]{1,0:T(8,128)(2,1)}, u32[]{:S(2)}) copy-start(bf16[1536,768]{1,0:T(8,128)(2,1)} %get-tuple-element.72.w_ref) | copy-start | bytes 7077892 | tf_op jit(solution)/shard_map/cond
  1.3 16.2 %copy-start.18 = (s32[2,4]{1,0:T(2,128)S(1)}, s32[2,4]{1,0:T(2,128)}, u32[]{:S(2)}) copy-start(s32[2,4]{1,0:T(2,128)} %get-tuple-element.70.lengths_ref) | copy-start | bytes 100 | tf_op jit(solution)/shard_map/cond
  11.9 4.6 %collective-permute-start.14 = (bf16[256,1536]{1,0:T(8,128)(2,1)}, bf16[256,1536]{1,0:T(8,128)(2,1)}, u32[]{:S(2)}, u32[]{:S(2)}) collective-permute-start(bf16[256,1536]{1,0:T(8,128)(2,1)} %section_forward.6), channel_id=1, source_target_pairs={{0,16},{1,17},{2,18},{3,19},{4,20},{5,21},{6,22},{7,23},{8,24},{9,... | collective-permute-start | bytes 2359304 | tf_op jit(solution)/shard_map/cond/branch_2_fun/ppermute | solution.py:252
  17.5 18.7 %copy-start.10 = (bf16[256,1536]{1,0:T(8,128)(2,1)S(1)}, bf16[256,1536]{1,0:T(8,128)(2,1)}, u32[]{:S(2)}) copy-start(bf16[256,1536]{1,0:T(8,128)(2,1)} %get-tuple-element.73.d_ref) | copy-start | bytes 2359300 | tf_op jit(solution)/shard_map/cond
  31.4 4.9 %collective-permute-start.15 = (bf16[256,1536]{1,0:T(8,128)(2,1)}, bf16[256,1536]{1,0:T(8,128)(2,1)}, u32[]{:S(2)}, u32[]{:S(2)}) collective-permute-start(bf16[256,1536]{1,0:T(8,128)(2,1)} %section_input_grad.6), channel_id=1, source_target_pairs={{16,0},{17,1},{18,2},{19,3},{20,4},{21,5},{22,6},{23,7},{24,8},{25... | collective-permute-start | bytes 2359304 | tf_op jit(solution)/shard_map/cond/branch_2_fun/ppermute | solution.py:252
  32.6 53.0 %collective-permute-start.17 = (bf16[1536,768]{1,0:T(8,128)(2,1)S(1)}, bf16[1536,768]{1,0:T(8,128)(2,1)}, u32[]{:S(2)}, u32[]{:S(2)}) collective-permute-start(bf16[1536,768]{1,0:T(8,128)(2,1)S(1)} %copy-done.2), channel_id=1, source_target_pairs={{0,4},{1,5},{2,6},{3,7},{4,0},{5,1},{6,2},{7,3},{8,12},{9,13},{10,... | collective-permute-start | bytes 7077896 | tf_op jit(solution)/shard_map/cond/branch_2_fun/ppermute | solution.py:246
  54.1 52.5 %collective-permute-start.19 = (bf16[640,768]{1,0:T(8,128)(2,1)}, bf16[640,768]{1,0:T(8,128)(2,1)S(1)}, u32[]{:S(2)}, u32[]{:S(2)}) collective-permute-start(bf16[640,768]{1,0:T(8,128)(2,1)} %get-tuple-element.77.l_ref), channel_id=1, source_target_pairs={{0,4},{1,5},{2,6},{3,7},{4,0},{5,1},{6,2},{7,3},{8,12},{9,13},{10,... | collective-permute-start | bytes 2949128 | tf_op jit(solution)/shard_map/cond/branch_2_fun/ppermute | solution.py:246
  56.5 67.1 %collective-permute-start.18 = (bf16[512,768]{1,0:T(8,128)(2,1)}, bf16[512,768]{1,0:T(8,128)(2,1)}, u32[]{:S(2)}, u32[]{:S(2)}) collective-permute-start(bf16[512,768]{1,0:T(8,128)(2,1)} %get-tuple-element.76.l_ref), channel_id=1, source_target_pairs={{0,4},{1,5},{2,6},{3,7},{4,0},{5,1},{6,2},{7,3},{8,12},{9,13},{10,... | collective-permute-start | bytes 2359304 | tf_op jit(solution)/shard_map/cond/branch_2_fun/ppermute | solution.py:246
  56.6 75.5 %collective-permute-start.16 = (bf16[256,768]{1,0:T(8,128)(2,1)}, bf16[256,768]{1,0:T(8,128)(2,1)}, u32[]{:S(2)}, u32[]{:S(2)}) collective-permute-start(bf16[256,768]{1,0:T(8,128)(2,1)} %get-tuple-element.75.l_ref), channel_id=1, source_target_pairs={{0,4},{1,5},{2,6},{3,7},{4,0},{5,1},{6,2},{7,3},{8,12},{9,13},{10,... | collective-permute-start | bytes 1179656 | tf_op jit(solution)/shard_map/cond/branch_2_fun/ppermute | solution.py:246
  58.6 77.7 %collective-permute-start.20 = (bf16[128,768]{1,0:T(8,128)(2,1)}, bf16[128,768]{1,0:T(8,128)(2,1)}, u32[]{:S(2)}, u32[]{:S(2)}) collective-permute-start(bf16[128,768]{1,0:T(8,128)(2,1)} %get-tuple-element.128), channel_id=1, source_target_pairs={{0,4},{1,5},{2,6},{3,7},{4,0},{5,1},{6,2},{7,3},{8,12},{9,13},{10,... | collective-permute-start | bytes 589832 | tf_op jit(solution)/shard_map/cond/branch_2_fun/ppermute | solution.py:246
  106.6 0.9 copy-start.14
where the time goes:
time: 140 us; the launch traced here: 138 us
  waiting for transfers between devices  68.3 us (49%)
  Pallas kernels  53.1 us (38%)
  starting transfers between devices  11.5 us (8%)
  other arithmetic  3.06 us (2%)
    ppermute x5, waiting for transfers between devices, partner(): return lax.ppermute(value, axis, pairs)  65.9 us
    pallas_call x1, Pallas kernels, run_local(): pl.pallas_call(local_kernel, out_shape=[jax.ShapeDtypeStruct((size, width...  15.8 us
    pallas_call x1, Pallas kernels, run_input_grad(): pl.pallas_call(input_grad_kernel, out_shape=jax.ShapeDtypeStruct(x.shape,...  13.8 us
    pallas_call x4, Pallas kernels, run_combine(): pl.pallas_call(combine_kernel, out_shape=[whole, whole], grid=(size // bl...  12.9 us
    pallas_call x1, Pallas kernels, run_forward(): pl.pallas_call(forward_kernel, out_shape=jax.ShapeDtypeStruct(x.shape, BF...  10.6 us
    ppermute x5, starting transfers between devices, partner(): return lax.ppermute(value, axis, pairs)  6.9 us
    ppermute x2, starting transfers between devices, shifted(): lax.ppermute(value, axis, [(source, source + steps) for source in range(l...  4.58 us
  transfers between devices with their start and end apart: 7, of which 7 were waited for; matrix products, arithmetic and copies ran while one was open for 2% of the time, Pallas kernels for 19%

commit v1 on v0

--- a/solution.py
+++ b/solution.py
@@ -9,6 +9,8 @@
 
 HS = 128
 SHARES = (5, 4, 2, 1)
+ROWS_UNROLL = 4
+HEADS_UNROLL = 2
 
 
 F32 = jnp.float32
@@ -41,7 +43,7 @@
         scale = lax.rsqrt(jnp.mean(xf * xf, axis=1, keepdims=True) + 1e-06)
         n_ref[r, :] = (xf * scale).astype(BF16)
 
-    each_block(x_ref.shape[0], 32, rows)
+    each_block(x_ref.shape[0], 32, rows, ROWS_UNROLL)
 
 
 def weights_of(u_head, vis):
@@ -53,12 +55,12 @@
     return 256 if extent % 256 == 0 else HS
 
 
-def each_block(extent, size, body):
+def each_block(extent, size, body, unroll=1):
     def once(index, carry):
         body(pl.ds(pl.multiple_of(index * size, size), size))
         return carry
 
-    lax.fori_loop(0, extent // size, once, 0)
+    lax.fori_loop(0, extent // size, once, 0, unroll=unroll)
 
 
 def project(out_ref, left_ref, w_ref):
@@ -77,7 +79,7 @@
         for micro in range(micros):
             body(slice(micro * rows, (micro + 1) * rows), c, masks[micro])
 
-    each_block(width, HS, heads)
+    each_block(width, HS, heads, HEADS_UNROLL)
 
 
 def forward_kernel(lengths_ref, x_ref, w_ref, out_ref, n_ref, u_ref, a_ref):
@@ -132,7 +134,7 @@
         dx = scale * dn - xf * (scale * scale * scale * along)
         out_ref[r, :] = (d_ref[r, :].astype(F32) + dx).astype(BF16)
 
-    each_block(x_ref.shape[0], 32, rows)
+    each_block(x_ref.shape[0], 32, rows, ROWS_UNROLL)
 
 
 def local_kernel(lengths_ref, x_ref, d_ref, w_ref, m_ref, *rest):

time: 140 us -> 137 us (0.979)
  Pallas kernels: 53.1 us -> 47.2 us
  waiting for transfers between devices: 68.3 us -> 71.2 us
    pallas_call x1, Pallas kernels: 15.8 us -> 12.9 us  [run_local(): pl.pallas_call(local_kernel, out_shape=[jax.ShapeDtypeStruct((size, width...]
    ppermute x5, waiting for transfers between devices: 65.9 us -> 68.7 us  [partner(): return lax.ppermute(value, axis, pairs)]
    pallas_call x1, Pallas kernels: 13.8 us -> 11.8 us  [run_input_grad(): pl.pallas_call(input_grad_kernel, out_shape=jax.ShapeDtypeStruct(x.shape,...]
  transfers between devices with their start and end apart: 7 -> 7, of which waited for: 7 -> 7; matrix products, arithmetic and copies ran while one was open for 2% -> 2% of each run, Pallas kernels for 19% -> 18%
where the time goes in v1:
time: 137 us; the launch traced here: 136 us
  waiting for transfers between devices  71.2 us (52%)
  Pallas kernels  47.2 us (34%)
  starting transfers between devices  11.5 us (8%)
  other arithmetic  3.06 us (2%)
    ppermute x5, waiting for transfers between devices, partner(): return lax.ppermute(value, axis, pairs)  68.7 us
    pallas_call x1, Pallas kernels, run_local(): pl.pallas_call(local_kernel, out_shape=[jax.ShapeDtypeStruct((size, width...  12.9 us
    pallas_call x4, Pallas kernels, run_combine(): pl.pallas_call(combine_kernel, out_shape=[whole, whole], grid=(size // bl...  12.9 us
    pallas_call x1, Pallas kernels, run_input_grad(): pl.pallas_call(input_grad_kernel, out_shape=jax.ShapeDtypeStruct(x.shape,...  11.8 us
    pallas_call x1, Pallas kernels, run_forward(): pl.pallas_call(forward_kernel, out_shape=jax.ShapeDtypeStruct(x.shape, BF...  9.6 us
    ppermute x5, starting transfers between devices, partner(): return lax.ppermute(value, axis, pairs)  6.9 us
    ppermute x2, starting transfers between devices, shifted(): lax.ppermute(value, axis, [(source, source + steps) for source in range(l...  4.59 us
  transfers between devices with their start and end apart: 7, of which 7 were waited for; matrix products, arithmetic and copies ran while one was open for 2% of the time, Pallas kernels for 18%

profile of v1, /device:TPU:0, one launch (start us, length us, event | category | flops | bytes accessed | tf_op | source)
XLA Modules:
  0.0 135.5 jit_solution(14687961333843867444)
XLA Ops:
  1.3 132.2 %conditional.1 = (bf16[1536,768]{1,0:T(8,128)(2,1)}, bf16[1536,768]{1,0:T(8,128)(2,1)}, bf16[128,768]{1,0:T(8,128)(2,1)}, bf16[128,768]{1,0:T(8,128)(2,1)}, bf16[1536,768]{1,0:T(8,128)(2,1)}) conditional(s32[]{:T(128)} %clamp.3, (s32[2,4]{1,0:T(2,128)}, bf16[256,1536]{1,0:T(8,128)(2,1)}, bf16[1536,768]{1,0:T(8,128)(2,1)}, ...), branch_computations={%region_0.1_spmd, %region_1.2_spmd, %region_2.3_spmd, %region_3.4_... | conditional | flops 5445255168 | bytes 79823488 | solution.py:282
  1.6 9.6 %section_forward.6 = bf16[256,1536]{1,0:T(8,128)(2,1)} custom-call(s32[2,4]{1,0:T(2,128)} %get-tuple-element.70.lengths_ref, bf16[256,1536]{1,0:T(8,128)(2,1)} %get-tuple-element.71.x_ref, bf16[1536,768]{1,0:T(8,128)(2,1)} %get-tuple-element.72.w_ref), custom_call_target="tpu_custom_call" | custom-call | flops 1207959552 | bytes 3932160 | tf_op jit(solution)/shard_map/cond/branch_2_fun/section_forward/pallas_call | solution.py:188
  11.2 3.3 %collective-permute-start.14 = (bf16[256,1536]{1,0:T(8,128)(2,1)}, bf16[256,1536]{1,0:T(8,128)(2,1)}, u32[]{:S(2)}, u32[]{:S(2)}) collective-permute-start(bf16[256,1536]{1,0:T(8,128)(2,1)} %section_forward.6), channel_id=1, source_target_pairs={{0,16},{1,17},{2,18},{3,19},{4,20},{5,21},{6,22},{7,23},{8,24},{9,... | collective-permute-start | bytes 2359304 | tf_op jit(solution)/shard_map/cond/branch_2_fun/ppermute | solution.py:254
  14.5 1.3 collective-permute-done.14
  15.8 1.0 broadcast_select_fusion.5.x_ref
  16.8 11.8 %section_input_grad.6 = bf16[256,1536]{1,0:T(8,128)(2,1)} custom-call(s32[2,4]{1,0:T(2,128)S(1)} %copy-done.18, bf16[256,1536]{1,0:T(8,128)(2,1)} %broadcast_select_fusion.5.x_ref, bf16[256,1536]{1,0:T(8,128)(2,1)} %get-tuple-element.73.d_ref, bf16[1536,768]{1,0:T(8,128)(2,1)S(1)} %copy-done.2), custom_call_target="tpu_custom_call" | custom-call | flops 1811939328 | bytes 4718592 | tf_op jit(solution)/shard_map/cond/branch_2_fun/section_input_grad/pallas_call | solution.py:201
  28.6 1.3 collective-permute-start.15
  29.9 2.5 %collective-permute-start.17 = (bf16[1536,768]{1,0:T(8,128)(2,1)S(1)}, bf16[1536,768]{1,0:T(8,128)(2,1)}, u32[]{:S(2)}, u32[]{:S(2)}) collective-permute-start(bf16[1536,768]{1,0:T(8,128)(2,1)S(1)} %copy-done.2), channel_id=1, source_target_pairs={{0,4},{1,5},{2,6},{3,7},{4,0},{5,1},{6,2},{7,3},{8,12},{9,13},{10,... | collective-permute-start | bytes 7077896 | tf_op jit(solution)/shard_map/cond/branch_2_fun/ppermute | solution.py:248
  32.3 1.1 collective-permute-done.15
  33.5 2.1 %broadcast_select_fusion.4.d_ref = bf16[256,1536]{1,0:T(8,128)(2,1)} fusion(bf16[256,1536]{1,0:T(8,128)(2,1)} %collective-permute-done.15, bf16[256,1536]{1,0:T(8,128)(2,1)S(1)} %copy-done.10, pred[]{:T(512)S(6)} %eq.23), kind=kLoop, calls=%fused_computation.4 | loop fusion | flops 393216 | bytes 2359297 | tf_op jit(solution)/shard_map/cond/branch_2_fun/jit(_where)/select_n | solution.py:268
  35.6 12.9 %section_local.6 = (bf16[640,768]{1,0:T(8,128)(2,1)}, bf16[512,768]{1,0:T(8,128)(2,1)}, bf16[256,768]{1,0:T(8,128)(2,1)}, bf16[128,768]{1,0:T(8,128)(2,1)}) custom-call(s32[2,4]{1,0:T(2,128)S(1)} %copy-done.18, bf16[256,1536]{1,0:T(8,128)(2,1)} %broadcast_select_fusion.5.x_ref, bf16[256,1536]{1,0:T(8,128)(2,1)} %broadcast_select_fusion.4.d_ref, ...), custom_call_target="tpu_custom_call" | custom-call | flops 2415919104 | bytes 8650752 | tf_op jit(solution)/shard_map/cond/branch_2_fun/section_local/pallas_call | solution.py:215
  48.5 2.4 %collective-permute-start.19 = (bf16[640,768]{1,0:T(8,128)(2,1)}, bf16[640,768]{1,0:T(8,128)(2,1)S(1)}, u32[]{:S(2)}, u32[]{:S(2)}) collective-permute-start(bf16[640,768]{1,0:T(8,128)(2,1)} %get-tuple-element.77.l_ref), channel_id=1, source_target_pairs={{0,4},{1,5},{2,6},{3,7},{4,0},{5,1},{6,2},{7,3},{8,12},{9,13},{10,... | collective-permute-start | bytes 2949128 | tf_op jit(solution)/shard_map/cond/branch_2_fun/ppermute | solution.py:248
  50.9 0.0 collective-permute-start.18
  50.9 2.0 %collective-permute-start.16 = (bf16[256,768]{1,0:T(8,128)(2,1)}, bf16[256,768]{1,0:T(8,128)(2,1)}, u32[]{:S(2)}, u32[]{:S(2)}) collective-permute-start(bf16[256,768]{1,0:T(8,128)(2,1)} %get-tuple-element.75.l_ref), channel_id=1, source_target_pairs={{0,4},{1,5},{2,6},{3,7},{4,0},{5,1},{6,2},{7,3},{8,12},{9,13},{10,... | collective-permute-start | bytes 1179656 | tf_op jit(solution)/shard_map/cond/branch_2_fun/ppermute | solution.py:248
  52.9 30.0 %collective-permute-done.17.wp_ref = bf16[1536,768]{1,0:T(8,128)(2,1)} collective-permute-done((bf16[1536,768]{1,0:T(8,128)(2,1)S(1)}, bf16[1536,768]{1,0:T(8,128)(2,1)}, u32[]{:S(2)}, u32[]{:S(2)}) %collective-permute-start.17) | collective-permute-done | bytes 2359328 | tf_op jit(solution)/shard_map/cond/branch_2_fun/ppermute | solution.py:248
  82.9 21.0 %collective-permute-done.19.lp_ref = bf16[640,768]{1,0:T(8,128)(2,1)S(1)} collective-permute-done((bf16[640,768]{1,0:T(8,128)(2,1)}, bf16[640,768]{1,0:T(8,128)(2,1)S(1)}, u32[]{:S(2)}, u32[]{:S(2)}) %collective-permute-start.19) | collective-permute-done | bytes 983072 | tf_op jit(solution)/shard_map/cond/branch_2_fun/ppermute | solution.py:248
  103.9 0.9 copy-done.14
  104.8 4.8 %combine.19 = (bf16[1536,768]{1,0:T(8,128)(2,1)}, bf16[1536,768]{1,0:T(8,128)(2,1)}) custom-call(bf16[640,768]{1,0:T(8,128)(2,1)} %get-tuple-element.77.l_ref, bf16[640,768]{1,0:T(8,128)(2,1)} %copy-done.14, bf16[1536,768]{1,0:T(8,128)(2,1)S(1)} %copy-done.2, bf16[1536,768]{1,0:T(8,128)(2,1)} %collective-permute-done.17.wp_ref), custom_call_target="tpu_custom_call" | custom-call | flops 3932160 | bytes 5898240 | tf_op jit(solution)/shard_map/cond/branch_2_fun/combine/pallas_call | solution.py:233
  109.6 11.2 %collective-permute-done.18.lp_ref = bf16[512,768]{1,0:T(8,128)(2,1)} collective-permute-done((bf16[512,768]{1,0:T(8,128)(2,1)}, bf16[512,768]{1,0:T(8,128)(2,1)}, u32[]{:S(2)}, u32[]{:S(2)}) %collective-permute-start.18) | collective-permute-done | bytes 786464 | tf_op jit(solution)/shard_map/cond/branch_2_fun/ppermute | solution.py:248
  120.8 3.9 %combine.20 = (bf16[1536,768]{1,0:T(8,128)(2,1)}, bf16[1536,768]{1,0:T(8,128)(2,1)}) custom-call(bf16[512,768]{1,0:T(8,128)(2,1)} %get-tuple-element.76.l_ref, bf16[512,768]{1,0:T(8,128)(2,1)} %collective-permute-done.18.lp_ref, bf16[1536,768]{1,0:T(8,128)(2,1)S(1)} %copy-done.2, ...), custom_call_target="tpu_custom_call", output_to_operand_aliasing={{0}: (4, {}), {1}: (5, {})} | custom-call | flops 3145728 | bytes 4718592 | tf_op jit(solution)/shard_map/cond/branch_2_fun/combine/pallas_call | solution.py:233
  124.7 4.5 %collective-permute-done.16.lp_ref = bf16[256,768]{1,0:T(8,128)(2,1)} collective-permute-done((bf16[256,768]{1,0:T(8,128)(2,1)}, bf16[256,768]{1,0:T(8,128)(2,1)}, u32[]{:S(2)}, u32[]{:S(2)}) %collective-permute-start.16) | collective-permute-done | bytes 393248 | tf_op jit(solution)/shard_map/cond/branch_2_fun/ppermute | solution.py:248
  129.3 2.2 %combine.21 = (bf16[1536,768]{1,0:T(8,128)(2,1)}, bf16[1536,768]{1,0:T(8,128)(2,1)}) custom-call(bf16[256,768]{1,0:T(8,128)(2,1)} %get-tuple-element.75.l_ref, bf16[256,768]{1,0:T(8,128)(2,1)} %collective-permute-done.16.lp_ref, bf16[1536,768]{1,0:T(8,128)(2,1)S(1)} %copy-done.2, ...), custom_call_target="tpu_custom_call", output_to_operand_aliasing={{0}: (4, {}), {1}: (5, {})} | custom-call | flops 1572864 | bytes 2359296 | tf_op jit(solution)/shard_map/cond/branch_2_fun/combine/pallas_call | solution.py:233
  131.4 2.0 %collective-permute-done.20 = bf16[128,768]{1,0:T(8,128)(2,1)} collective-permute-done((bf16[128,768]{1,0:T(8,128)(2,1)}, bf16[128,768]{1,0:T(8,128)(2,1)}, u32[]{:S(2)}, u32[]{:S(2)}) %collective-permute-start.20) | collective-permute-done | bytes 196640 | tf_op jit(solution)/shard_map/cond/branch_2_fun/ppermute | solution.py:248
  133.5 2.1 %combine.25 = (bf16[1536,768]{1,0:T(8,128)(2,1)}, bf16[1536,768]{1,0:T(8,128)(2,1)}) custom-call(bf16[128,768]{1,0:T(8,128)(2,1)} %get-tuple-element.109.l_ref, bf16[128,768]{1,0:T(8,128)(2,1)} %get-tuple-element.110.lp_ref, bf16[1536,768]{1,0:T(8,128)(2,1)} %bitcast.15, ...), custom_call_target="tpu_custom_call", output_to_operand_aliasing={{0}: (4, {}), {1}: (5, {})} | custom-call | flops 786432 | bytes 1179648 | tf_op jit(solution)/shard_map/combine/pallas_call | solution.py:233
  (10 shorter events, 0.0 us)
Async XLA Ops:
  1.5 14.3 %copy-start.6 = (bf16[256,1536]{1,0:T(8,128)(2,1)S(1)}, bf16[256,1536]{1,0:T(8,128)(2,1)}, u32[]{:S(2)}) copy-start(bf16[256,1536]{1,0:T(8,128)(2,1)} %get-tuple-element.71.x_ref) | copy-start | bytes 2359300 | tf_op jit(solution)/shard_map/cond
  1.6 15.2 %copy-start.2 = (bf16[1536,768]{1,0:T(8,128)(2,1)S(1)}, bf16[1536,768]{1,0:T(8,128)(2,1)}, u32[]{:S(2)}) copy-start(bf16[1536,768]{1,0:T(8,128)(2,1)} %get-tuple-element.72.w_ref) | copy-start | bytes 7077892 | tf_op jit(solution)/shard_map/cond
  1.6 15.2 %copy-start.18 = (s32[2,4]{1,0:T(2,128)S(1)}, s32[2,4]{1,0:T(2,128)}, u32[]{:S(2)}) copy-start(s32[2,4]{1,0:T(2,128)} %get-tuple-element.70.lengths_ref) | copy-start | bytes 100 | tf_op jit(solution)/shard_map/cond
  11.2 4.6 %collective-permute-start.14 = (bf16[256,1536]{1,0:T(8,128)(2,1)}, bf16[256,1536]{1,0:T(8,128)(2,1)}, u32[]{:S(2)}, u32[]{:S(2)}) collective-permute-start(bf16[256,1536]{1,0:T(8,128)(2,1)} %section_forward.6), channel_id=1, source_target_pairs={{0,16},{1,17},{2,18},{3,19},{4,20},{5,21},{6,22},{7,23},{8,24},{9,... | collective-permute-start | bytes 2359304 | tf_op jit(solution)/shard_map/cond/branch_2_fun/ppermute | solution.py:254
  16.8 16.7 %copy-start.10 = (bf16[256,1536]{1,0:T(8,128)(2,1)S(1)}, bf16[256,1536]{1,0:T(8,128)(2,1)}, u32[]{:S(2)}) copy-start(bf16[256,1536]{1,0:T(8,128)(2,1)} %get-tuple-element.73.d_ref) | copy-start | bytes 2359300 | tf_op jit(solution)/shard_map/cond
  28.6 4.9 %collective-permute-start.15 = (bf16[256,1536]{1,0:T(8,128)(2,1)}, bf16[256,1536]{1,0:T(8,128)(2,1)}, u32[]{:S(2)}, u32[]{:S(2)}) collective-permute-start(bf16[256,1536]{1,0:T(8,128)(2,1)} %section_input_grad.6), channel_id=1, source_target_pairs={{16,0},{17,1},{18,2},{19,3},{20,4},{21,5},{22,6},{23,7},{24,8},{25... | collective-permute-start | bytes 2359304 | tf_op jit(solution)/shard_map/cond/branch_2_fun/ppermute | solution.py:254
  29.9 53.0 %collective-permute-start.17 = (bf16[1536,768]{1,0:T(8,128)(2,1)S(1)}, bf16[1536,768]{1,0:T(8,128)(2,1)}, u32[]{:S(2)}, u32[]{:S(2)}) collective-permute-start(bf16[1536,768]{1,0:T(8,128)(2,1)S(1)} %copy-done.2), channel_id=1, source_target_pairs={{0,4},{1,5},{2,6},{3,7},{4,0},{5,1},{6,2},{7,3},{8,12},{9,13},{10,... | collective-permute-start | bytes 7077896 | tf_op jit(solution)/shard_map/cond/branch_2_fun/ppermute | solution.py:248
  48.5 55.4 %collective-permute-start.19 = (bf16[640,768]{1,0:T(8,128)(2,1)}, bf16[640,768]{1,0:T(8,128)(2,1)S(1)}, u32[]{:S(2)}, u32[]{:S(2)}) collective-permute-start(bf16[640,768]{1,0:T(8,128)(2,1)} %get-tuple-element.77.l_ref), channel_id=1, source_target_pairs={{0,4},{1,5},{2,6},{3,7},{4,0},{5,1},{6,2},{7,3},{8,12},{9,13},{10,... | collective-permute-start | bytes 2949128 | tf_op jit(solution)/shard_map/cond/branch_2_fun/ppermute | solution.py:248
  50.9 69.9 %collective-permute-start.18 = (bf16[512,768]{1,0:T(8,128)(2,1)}, bf16[512,768]{1,0:T(8,128)(2,1)}, u32[]{:S(2)}, u32[]{:S(2)}) collective-permute-start(bf16[512,768]{1,0:T(8,128)(2,1)} %get-tuple-element.76.l_ref), channel_id=1, source_target_pairs={{0,4},{1,5},{2,6},{3,7},{4,0},{5,1},{6,2},{7,3},{8,12},{9,13},{10,... | collective-permute-start | bytes 2359304 | tf_op jit(solution)/shard_map/cond/branch_2_fun/ppermute | solution.py:248
  50.9 78.3 %collective-permute-start.16 = (bf16[256,768]{1,0:T(8,128)(2,1)}, bf16[256,768]{1,0:T(8,128)(2,1)}, u32[]{:S(2)}, u32[]{:S(2)}) collective-permute-start(bf16[256,768]{1,0:T(8,128)(2,1)} %get-tuple-element.75.l_ref), channel_id=1, source_target_pairs={{0,4},{1,5},{2,6},{3,7},{4,0},{5,1},{6,2},{7,3},{8,12},{9,13},{10,... | collective-permute-start | bytes 1179656 | tf_op jit(solution)/shard_map/cond/branch_2_fun/ppermute | solution.py:248
  52.9 80.6 %collective-permute-start.20 = (bf16[128,768]{1,0:T(8,128)(2,1)}, bf16[128,768]{1,0:T(8,128)(2,1)}, u32[]{:S(2)}, u32[]{:S(2)}) collective-permute-start(bf16[128,768]{1,0:T(8,128)(2,1)} %get-tuple-element.128), channel_id=1, source_target_pairs={{0,4},{1,5},{2,6},{3,7},{4,0},{5,1},{6,2},{7,3},{8,12},{9,13},{10,... | collective-permute-start | bytes 589832 | tf_op jit(solution)/shard_map/cond/branch_2_fun/ppermute | solution.py:248
  103.9 0.9 copy-start.14
